TPU v7x, 256 devices: a whole 4x4x8 slice. The times are simulated.
256 devices in a mesh: dp: 2 (over core), row: 16 (over y, x), col: 8 (over z).
Axes of the slice: x: 4, y: 4, z: 8, core: 2. Of those that a mesh axis runs over, the one named last changes fastest.
Arguments:
- features: bfloat16 [256, 96, 2048], P(('dp', 'row'), 'col'), parts along dimension 0, may hold values from 0 to 40
- low_level: bfloat16 [512, 192, 256], P(('dp', 'row'), 'col'), parts along dimension 0, may hold values from -6 to 6
- point_weight: bfloat16 [2048, 256], P(None, 'row'), may hold values from -0.125 to 0.125
- atrous_weight: bfloat16 [3, 3, 3, 2048, 256], P(None, None, None, None, 'row'), may hold values from -0.046875 to 0.046875
- pool_weight: bfloat16 [2048, 256], P(None, 'row'), may hold values from -0.125 to 0.125
- aspp_bias: float32 [5, 256], P(None, 'row'), may hold values from -1.5 to 1.5
- proj_weight: bfloat16 [1280, 256], replicated, may hold values from -0.15625 to 0.15625
- proj_bias: float32 [256], replicated, may hold values from -1.5 to 1.5
- low_weight: bfloat16 [256, 48], replicated, may hold values from -0.375 to 0.375
- low_bias: float32 [48], replicated, may hold values from -1.5 to 1.5
- conv1_weight: bfloat16 [3, 3, 304, 256], replicated, may hold values from -0.109375 to 0.109375
- conv1_bias: float32 [256], replicated, may hold values from -1.5 to 1.5
- conv2_weight: bfloat16 [3, 3, 256, 256], replicated, may hold values from -0.125 to 0.125
- conv2_bias: float32 [256], replicated, may hold values from -1.5 to 1.5
Outputs:
- decoded: bfloat16 [512, 192, 256], P(('dp', 'row'), 'col'), parts along dimension 0
There are 2 independent parts, one for each index of `dp`. A program takes and returns all parts, laid end to end along the dimension named above; an argument that names none is the same for every part. Nothing has to cross between parts.
All inputs are finite; a program needn't handle non-finite values.
Results may differ from a plain program's by a relative error of at most 0.0057.
Values may be sent and summed in bfloat16 or wider, within the bound.
No kernel may reach another device: no remote copies, remote signals or barrier semaphores. Data moves between devices by JAX's collectives and lax.ppermute only.
A program may use at most 128 MiB of HBM per device.

v0:
```python
import jax
import jax.numpy as jnp
from jax import lax
from jax.sharding import Mesh
from jax.sharding import PartitionSpec as P

ROW = ("row_0", "row_1")
ROW_COL = ("row_0", "row_1", "col")
DP_ROW = ("dp", "row_0", "row_1")
RATES = (12, 24, 36)


def from_behind(value, axis, by):
    devices = lax.axis_size(axis)
    pairs = [(i, i + by) for i in range(devices) if 0 <= i + by < devices]
    return lax.ppermute(value, axis, pairs)


def one_axis_at_a_time(value, axes):
    for axis in axes:
        value = lax.psum(value, axis)
    return value


def padded_2(value, sides, width):
    for axis, dim in sides:
        devices, length = (lax.axis_size(axis), value.shape[dim])
        up = [(i, (i + 1) % devices) for i in range(devices - 1)]
        down = [(j, i) for i, j in up]
        last = lax.slice_in_dim(value, length - width, length, axis=dim)
        first = lax.slice_in_dim(value, 0, width, axis=dim)
        before = lax.ppermute(last, axis, up)
        after = lax.ppermute(first, axis, down)
        value = jnp.concatenate([before, value, after], axis=dim)
    return value


def enlarge(padded):
    values = padded.astype(jnp.float32)
    middle = values[1:-1]
    even = 0.75 * middle + 0.25 * values[:-2]
    odd = 0.75 * middle + 0.25 * values[2:]
    values = jnp.stack([even, odd], axis=1).reshape(
        2 * middle.shape[0], middle.shape[1], middle.shape[2]
    )
    middle = values[:, 1:-1]
    even = 0.75 * middle + 0.25 * values[:, :-2]
    odd = 0.75 * middle + 0.25 * values[:, 2:]
    values = jnp.stack([even, odd], axis=2).reshape(
        values.shape[0], 2 * middle.shape[1], middle.shape[2]
    )
    return values.astype(jnp.bfloat16)


def convolve(padded, weight, bias):
    height, width = (padded.shape[0] - 2, padded.shape[1] - 2)
    windows = []
    for row_tap in range(3):
        for col_tap in range(3):
            windows.append(padded[row_tap : row_tap + height, col_tap : col_tap + width])
    columns = jnp.concatenate(windows, axis=2)
    depth = columns.shape[2]
    result = jnp.dot(
        columns.reshape(-1, depth), weight.reshape(depth, -1), preferred_element_type=jnp.float32
    )
    result = jnp.maximum(result + bias, 0.0).astype(jnp.bfloat16)
    return result.reshape(height, width, -1)


def local_rows(values, offset):
    height = values.shape[0]
    extent = abs(offset)
    padded = jnp.pad(values, ((extent, extent), (0, 0), (0, 0)))
    return padded[extent + offset : extent + offset + height]


def bring_cols(values, steps):
    if steps == 0:
        return values
    return from_behind(values, "col", steps)


def move_cols(values, distance):
    width = values.shape[1]
    whole = distance // width
    pieces = bring_cols(values, -whole)
    return pieces


def fix_edges(padded, at_start, at_end, axis_number):
    size = padded.shape[axis_number]
    first = lax.slice_in_dim(padded, 0, 1, axis=axis_number)
    second = lax.slice_in_dim(padded, 1, 2, axis=axis_number)
    middle = lax.slice_in_dim(padded, 1, size - 1, axis=axis_number)
    before = lax.slice_in_dim(padded, size - 2, size - 1, axis=axis_number)
    final = lax.slice_in_dim(padded, size - 1, size, axis=axis_number)
    first = jnp.where(at_start, second, first)
    final = jnp.where(at_end, before, final)
    return jnp.concatenate([first, middle, final], axis=axis_number)


def on_device(
    features,
    low_level,
    point_weight,
    atrous_weight,
    pool_weight,
    aspp_bias,
    proj_weight,
    proj_bias,
    low_weight,
    low_bias,
    conv1_weight,
    conv1_bias,
    conv2_weight,
    conv2_bias,
):
    in_width = features.shape[2]
    own_width = point_weight.shape[1]
    out_width = proj_weight.shape[1]
    row_count = lax.axis_size(ROW)
    col_count = lax.axis_size("col")
    row_index = lax.axis_index(ROW)
    col_index = lax.axis_index("col")
    tile_rows, tile_cols = (features.shape[0], features.shape[1])
    full_rows = tile_rows * row_count
    full_cols = tile_cols * col_count
    atrous_flat = jnp.transpose(atrous_weight.reshape(27, in_width, own_width), (1, 0, 2)).reshape(
        in_width, 27 * own_width
    )
    own_stack = jnp.concatenate([point_weight, atrous_flat, pool_weight], axis=1)
    group_total = 28
    stacked = own_stack[:, : group_total * own_width]
    piece = lax.all_gather(features, ROW, axis=0, tiled=True)
    result = jnp.dot(piece.reshape(-1, in_width), stacked, preferred_element_type=jnp.float32)
    products = result.reshape(piece.shape[0], piece.shape[1], -1)
    map_rows = products.shape[0]

    def group(number):
        return products[:, :, number * own_width : (number + 1) * own_width]

    all_width = own_width * row_count
    first_col = jnp.where(col_index == 0, 1.0, 0.0).astype(jnp.float32)
    spread_bias = lax.dynamic_update_slice_in_dim(
        jnp.zeros((5, all_width), jnp.float32), aspp_bias * first_col, row_index * own_width, 1
    )
    tile_sum = jnp.sum(features.astype(jnp.float32), axis=(0, 1))
    scene_sum, full_bias = (
        one_axis_at_a_time(tile_sum, ROW_COL),
        one_axis_at_a_time(spread_bias, ROW_COL),
    )
    pooled = jnp.dot(
        scene_sum, pool_weight.astype(jnp.float32), precision=lax.Precision.HIGHEST
    ) / (full_rows * full_cols)
    last_axis = full_bias.ndim - 1
    bias_mine = lax.dynamic_slice_in_dim(full_bias, row_index * own_width, own_width, last_axis)

    def activate(values, number):
        return jnp.maximum(values + bias_mine[number], 0.0).astype(jnp.bfloat16)

    outputs = [activate(group(0), 0)]
    for rate_number in range(3):
        dilation = RATES[rate_number]
        running = jnp.zeros((map_rows, tile_cols, own_width), jnp.float32)
        for col_tap in range(3):
            column_sum = jnp.zeros((map_rows, tile_cols, own_width), jnp.float32)
            for row_tap in range(3):
                row_values = group(1 + rate_number * 9 + row_tap * 3 + col_tap)
                offset = (row_tap - 1) * RATES[rate_number]
                column_sum = column_sum + local_rows(row_values, offset)
            running = running + move_cols(column_sum, (col_tap - 1) * dilation)
        outputs.append(activate(running, rate_number + 1))
    pool_branch = jnp.maximum(pooled + bias_mine[4], 0.0).astype(jnp.bfloat16)
    outputs.append(jnp.broadcast_to(pool_branch, (map_rows, tile_cols, own_width)))
    branches = jnp.concatenate(outputs, axis=2)
    blocks = proj_weight.reshape(5, row_count, own_width, out_width)
    swapped = lax.all_to_all(branches, ROW, split_axis=0, concat_axis=2, tiled=True)
    reordered = jnp.transpose(blocks, (1, 0, 2, 3)).reshape(-1, out_width)
    summed = jnp.dot(
        swapped.reshape(-1, swapped.shape[2]), reordered, preferred_element_type=jnp.float32
    )
    coarse = (
        jnp.maximum(summed + proj_bias, 0.0)
        .astype(jnp.bfloat16)
        .reshape(tile_rows, tile_cols, out_width)
    )
    padded = padded_2(coarse, ((ROW, 0), ("col", 1)), 1)
    padded = fix_edges(padded, row_index == 0, row_index == row_count - 1, 0)
    padded = fix_edges(padded, col_index == 0, col_index == col_count - 1, 1)
    upsampled = enlarge(padded)
    low_rows = low_level.reshape(-1, low_level.shape[2])
    reduced = jnp.dot(low_rows, low_weight, preferred_element_type=jnp.float32)
    reduced = (
        jnp.maximum(reduced + low_bias, 0.0)
        .astype(jnp.bfloat16)
        .reshape(low_level.shape[0], low_level.shape[1], -1)
    )
    joined_fine = jnp.concatenate([upsampled, reduced], axis=2)
    padded_fine = padded_2(joined_fine, ((ROW, 0), ("col", 1)), 1)
    hidden = convolve(padded_fine, conv1_weight, conv1_bias)
    padded_hidden = padded_2(hidden, ((ROW, 0), ("col", 1)), 1)
    return convolve(padded_hidden, conv2_weight, conv2_bias)


def solution(mesh):
    torus = Mesh(
        mesh.devices.reshape(mesh.shape["dp"], 4, 4, mesh.shape["col"]),
        ("dp", "row_0", "row_1", "col"),
    )
    placed = (
        P(DP_ROW, "col", None),
        P(DP_ROW, "col", None),
        P(None, ROW),
        P(None, None, None, None, ROW),
        P(None, ROW),
        P(None, ROW),
        P(),
        P(),
        P(),
        P(),
        P(),
        P(),
        P(),
        P(),
    )
    return jax.shard_map(
        on_device, mesh=torus, in_specs=placed, out_specs=P(DP_ROW, "col", None), check_vma=False
    )
```

profile of v0, /device:TPU:70, one launch (start us, length us, event | category | flops | bytes accessed | tf_op | source)
XLA Modules:
  0.0 292.7 jit_solution(2077303134434737102)
XLA Ops:
  9.2 17.2 %all-reduce.20 = (f32[5,256]{1,0:T(8,128)S(1)}, f32[2048]{0:T(1024)S(1)}) all-reduce(f32[5,256]{1,0:T(8,128)S(1)} %dynamic_update_slice.3, f32[2048]{0:T(1024)S(1)} %convert_reduce_fusion), channel_id=1, replica_groups=mesh['dp'=2,'row_0'=4,'row_1'=4,'col'=8] {'row_0'}, use_global_device_ids=true, to_apply=%region_0.1 | all-reduce | flops 3328 | bytes 26624 | tf_op jit(solution)/shard_map/psum | solution.py:21
  26.4 13.9 %all-reduce.19 = (f32[5,256]{1,0:T(8,128)S(1)}, f32[2048]{0:T(1024)S(1)}) all-reduce(f32[5,256]{1,0:T(8,128)S(1)} %get-tuple-element.9, f32[2048]{0:T(1024)S(1)} %get-tuple-element.10), channel_id=1, replica_groups=mesh['dp'=2,'row_0'=4,'row_1'=4,'col'=8] {'row_1'}, use_global_device_ids=true, to_apply=%region_1.2 | all-reduce | flops 3328 | bytes 26624 | tf_op jit(solution)/shard_map/psum | solution.py:21
  40.3 29.7 %all-reduce.18 = (f32[5,256]{1,0:T(8,128)S(1)}, f32[2048]{0:T(1024)S(1)}) all-reduce(f32[5,256]{1,0:T(8,128)S(1)} %get-tuple-element.7, f32[2048]{0:T(1024)S(1)} %get-tuple-element.8), channel_id=1, replica_groups=mesh['dp'=2,'row_0'=4,'row_1'=4,'col'=8] {'col'}, use_global_device_ids=true, to_apply=%region_2.3 | all-reduce | flops 3328 | bytes 26624 | tf_op jit(solution)/shard_map/psum | solution.py:21
  71.0 7.2 %all-gather.2.cloned.1.call-done = bf16[128,12,2048]{2,0,1:T(8,128)(2,1)} async-done(((bf16[8,12,2048]{2,0,1:T(8,128)(2,1)}), bf16[128,12,2048]{2,0,1:T(8,128)(2,1)}) %all-gather.2.cloned.1.call-update) | async-done | bytes 6291472 | tf_op jit(solution)/shard_map/all_gather | solution.py:134
  78.3 9.7 %copy.180 = bf16[128,12,2048]{2,1,0:T(8,128)(2,1)} copy(bf16[128,12,2048]{2,0,1:T(8,128)(2,1)} %all-gather.2.cloned.1.call-done) | data formatting | bytes 12582912 | tf_op jit(solution)/shard_map/all_gather | solution.py:134
  88.0 10.8 %reshape.87 = bf16[1536,2048]{1,0:T(8,128)(2,1)} reshape(bf16[128,12,2048]{2,1,0:T(8,128)(2,1)} %copy.180) | data formatting | bytes 12582912 | tf_op jit(solution)/shard_map/reshape | solution.py:135
  98.9 7.3 %convolution_bitcast_fusion = f32[1536,448]{0,1:T(8,128)} fusion(bf16[1536,2048]{1,0:T(8,128)(2,1)} %reshape.87, bf16[2048,432]{0,1:T(8,128)(2,1)S(1)} %bitcast.118, bf16[2048,16]{0,1:T(8,128)(2,1)S(1)} %copy-done.19), kind=kOutput, calls=%fused_computation | convolution fusion | flops 2822242304 | bytes 10878976 | tf_op jit(solution)/shard_map/dot_general | solution.py:135
  106.2 3.4 %copy.181 = f32[1536,448]{1,0:T(8,128)} copy(f32[1536,448]{0,1:T(8,128)} %convolution_bitcast_fusion) | data formatting | bytes 5505024 | tf_op jit(solution)/shard_map/dot_general | solution.py:135
  109.6 4.6 %reshape.88 = f32[128,12,448]{2,1,0:T(8,128)} reshape(f32[1536,448]{1,0:T(8,128)} %copy.181) | data formatting | bytes 5505024 | tf_op jit(solution)/shard_map/reshape | solution.py:136
  114.2 13.5 %fusion.61 = (f32[128,12,16]{2,1,0:T(8,128)}, f32[128,12,16]{2,1,0:T(8,128)}, f32[128,12,16]{2,1,0:T(8,128)}, f32[128,12,16]{2,1,0:T(8,128)}, f32[128,12,16]{2,1...) fusion(f32[128,12,448]{2,1,0:T(8,128)} %reshape.88), kind=kLoop, calls=%fused_computation.144 | loop fusion | bytes 3735552 | tf_op jit(solution)/shard_map/slice | solution.py:140
  145.1 8.7 %fusion.62 = (f32[128,12,16]{2,1,0:T(8,128)}, f32[128,12,16]{2,1,0:T(8,128)}, f32[128,12,16]{2,1,0:T(8,128)}, f32[128,12,16]{2,1,0:T(8,128)}, f32[128,12,16]{2,1...) fusion(f32[128,12,448]{2,1,0:T(8,128)} %reshape.88, ...), kind=kLoop, calls=%fused_computation.145 | loop fusion | flops 245760 | bytes 2555904 | tf_op jit(solution)/shard_map/slice | solution.py:140
  165.4 2.4 collective-permute-start.1
  167.8 6.6 %collective-permute-start.2 = (f32[128,12,16]{0,2,1:T(8,128)}, f32[128,12,16]{0,2,1:T(8,128)}, u32[]{:S(2)}, u32[]{:S(2)}) collective-permute-start(f32[128,12,16]{0,2,1:T(8,128)} %copy.188), channel_id=1, source_target_pairs={{0,2},{1,3},{2,4},{3,5},{4,6},{5,7},{8,10},{9,11},{10,12},{11,13},... | collective-permute-start | bytes 294920 | tf_op jit(solution)/shard_map/ppermute | solution.py:16
  174.4 6.7 %collective-permute-start.4 = (f32[128,12,16]{0,2,1:T(8,128)}, f32[128,12,16]{0,2,1:T(8,128)}, u32[]{:S(2)}, u32[]{:S(2)}) collective-permute-start(f32[128,12,16]{0,2,1:T(8,128)} %copy.193), channel_id=1, source_target_pairs={{0,3},{1,4},{2,5},{3,6},{4,7},{8,11},{9,12},{10,13},{11,14},{12,15... | collective-permute-start | bytes 294920 | tf_op jit(solution)/shard_map/ppermute | solution.py:16
  185.6 3.8 %collective-permute-start.3 = (f32[128,12,16]{0,2,1:T(8,128)}, f32[128,12,16]{0,2,1:T(8,128)S(1)}, u32[]{:S(2)}, u32[]{:S(2)}) collective-permute-start(f32[128,12,16]{0,2,1:T(8,128)} %copy.192), channel_id=1, source_target_pairs={{2,0},{3,1},{4,2},{5,3},{6,4},{7,5},{10,8},{11,9},{12,10},{13,11},... | collective-permute-start | bytes 294920 | tf_op jit(solution)/shard_map/ppermute | solution.py:16
  192.0 2.7 collective-permute-done.3
  201.7 5.7 %all-to-all-start = ((bf16[16,2,3840]{2,1,0:T(2,128)(2,1)}), bf16[16,2,3840]{2,1,0:T(2,128)(2,1)S(1)}, u32[]{:S(2)}, u32[]{:S(2)}) async-start(bf16[16,2,3840]{2,1,0:T(2,128)(2,1)} %reshape.102), calls=%async_computation | async-start | bytes 491520 | tf_op jit(solution)/shard_map/all_to_all | solution.py:177
  207.5 6.2 %all-to-all-done = bf16[16,2,3840]{2,1,0:T(2,128)(2,1)S(1)} async-done(((bf16[16,2,3840]{2,1,0:T(2,128)(2,1)}), bf16[16,2,3840]{2,1,0:T(2,128)(2,1)S(1)}, u32[]{:S(2)}, u32[]{:S(2)}) %all-to-all-start) | async-done | bytes 245792 | tf_op jit(solution)/shard_map/all_to_all | solution.py:177
  215.4 3.6 %collective-permute-start.6 = (bf16[1,12,256]{2,1,0:T(8,128)(2,1)S(1)}, bf16[1,12,256]{2,1,0:T(8,128)(2,1)S(1)}, u32[]{:S(2)}, u32[]{:S(2)}) collective-permute-start(bf16[1,12,256]{2,1,0:T(8,128)(2,1)S(1)} %get-tuple-element.77), channel_id=1, source_target_pairs={{0,8},{8,16},{16,24},{24,32},{32,40},{40,48},{48,56},{56,64},{64,7... | collective-permute-start | bytes 18440 | tf_op jit(solution)/shard_map/ppermute | solution.py:32
  221.4 5.4 %collective-permute-done.7 = bf16[1,12,256]{2,1,0:T(8,128)(2,1)S(1)} collective-permute-done((bf16[1,12,256]{2,1,0:T(8,128)(2,1)S(1)}, bf16[1,12,256]{2,1,0:T(8,128)(2,1)S(1)}, u32[]{:S(2)}, u32[]{:S(2)}) %collective-permute-start.7) | collective-permute-done | bytes 6176 | tf_op jit(solution)/shard_map/ppermute | solution.py:33
  228.7 3.9 %collective-permute-start.9 = (bf16[10,1,256]{2,1,0:T(2,128)(2,1)S(1)}, bf16[10,1,256]{2,1,0:T(2,128)(2,1)S(1)}, u32[]{:S(2)}, u32[]{:S(2)}) collective-permute-start(bf16[10,1,256]{2,1,0:T(2,128)(2,1)S(1)} %get-tuple-element.75), channel_id=1, source_target_pairs={{1,0},{2,1},{3,2},{4,3},{5,4},{6,5},{7,6},{9,8},{10,9},{11,10},{12... | collective-permute-start | bytes 15368 | tf_op jit(solution)/shard_map/ppermute | solution.py:33
  237.1 3.9 %collective-permute-start.11 = (bf16[1,24,304]{2,0,1:T(2,128)(2,1)S(1)}, bf16[1,24,304]{2,0,1:T(2,128)(2,1)S(1)}, u32[]{:S(2)}, u32[]{:S(2)}) collective-permute-start(bf16[1,24,304]{2,0,1:T(2,128)(2,1)S(1)} %get-tuple-element.57), channel_id=1, source_target_pairs={{8,0},{16,8},{24,16},{32,24},{40,32},{48,40},{56,48},{64,56},{72,6... | collective-permute-start | bytes 43784 | tf_op jit(solution)/shard_map/ppermute | solution.py:33
  242.0 3.1 %collective-permute-done.11 = bf16[1,24,304]{2,0,1:T(2,128)(2,1)S(1)} collective-permute-done((bf16[1,24,304]{2,0,1:T(2,128)(2,1)S(1)}, bf16[1,24,304]{2,0,1:T(2,128)(2,1)S(1)}, u32[]{:S(2)}, u32[]{:S(2)}) %collective-permute-start.11) | collective-permute-done | bytes 14624 | tf_op jit(solution)/shard_map/ppermute | solution.py:33
  245.1 4.1 %collective-permute-start.13 = (bf16[18,1,304]{2,0,1:T(8,128)(2,1)S(1)}, bf16[18,1,304]{2,0,1:T(8,128)(2,1)S(1)}, u32[]{:S(2)}, u32[]{:S(2)}) collective-permute-start(bf16[18,1,304]{2,0,1:T(8,128)(2,1)S(1)} %get-tuple-element.46), channel_id=1, source_target_pairs={{1,0},{2,1},{3,2},{4,3},{5,4},{6,5},{7,6},{9,8},{10,9},{11,10},{12... | collective-permute-start | bytes 32840 | tf_op jit(solution)/shard_map/ppermute | solution.py:33
  251.6 3.3 %collective-permute-done.12 = bf16[18,1,304]{2,0,1:T(8,128)(2,1)S(1)} collective-permute-done((bf16[18,1,304]{2,0,1:T(8,128)(2,1)S(1)}, bf16[18,1,304]{2,0,1:T(8,128)(2,1)S(1)}, u32[]{:S(2)}, u32[]{:S(2)}) %collective-permute-start.12) | collective-permute-done | bytes 10976 | tf_op jit(solution)/shard_map/ppermute | solution.py:32
  256.8 4.9 %concatenate.122 = bf16[384,2736]{1,0:T(8,128)(2,1)} concatenate(bf16[384,304]{1,0:T(8,128)(2,1)S(1)} %bitcast.104, bf16[384,304]{1,0:T(8,128)(2,1)S(1)} %bitcast.100, bf16[384,304]{1,0:T(8,128)(2,1)S(1)} %bitcast.103, bf16[384,304]{1,0:T(8,128)(2,1)S(1)} %bitcast.105, bf16[384,256]{1,0:T(8,128)(2,1)} %convert_element_type.76, bf16[384,48]{1,0:T(8,128)(2,1)} %copy-done.6, ...), dimensions={1} | concatenate | bytes 4202496 | tf_op jit(solution)/shard_map/concatenate | solution.py:61
  261.7 2.3 fusion.6
  266.0 3.9 %collective-permute-start.15 = (bf16[1,24,256]{2,1,0:T(8,128)(2,1)S(1)}, bf16[1,24,256]{2,1,0:T(8,128)(2,1)S(1)}, u32[]{:S(2)}, u32[]{:S(2)}) collective-permute-start(bf16[1,24,256]{2,1,0:T(8,128)(2,1)S(1)} %get-tuple-element.67), channel_id=1, source_target_pairs={{8,0},{16,8},{24,16},{32,24},{40,32},{48,40},{56,48},{64,56},{72,6... | collective-permute-start | bytes 36872 | tf_op jit(solution)/shard_map/ppermute | solution.py:33
  269.9 3.8 %collective-permute-done.15 = bf16[1,24,256]{2,1,0:T(8,128)(2,1)S(1)} collective-permute-done((bf16[1,24,256]{2,1,0:T(8,128)(2,1)S(1)}, bf16[1,24,256]{2,1,0:T(8,128)(2,1)S(1)}, u32[]{:S(2)}, u32[]{:S(2)}) %collective-permute-start.15) | collective-permute-done | bytes 12320 | tf_op jit(solution)/shard_map/ppermute | solution.py:33
  273.7 3.5 %collective-permute-start.17 = (bf16[18,1,256]{2,1,0:T(2,128)(2,1)S(1)}, bf16[18,1,256]{2,1,0:T(2,128)(2,1)S(1)}, u32[]{:S(2)}, u32[]{:S(2)}) collective-permute-start(bf16[18,1,256]{2,1,0:T(2,128)(2,1)S(1)} %get-tuple-element.62), channel_id=1, source_target_pairs={{1,0},{2,1},{3,2},{4,3},{5,4},{6,5},{7,6},{9,8},{10,9},{11,10},{12... | collective-permute-start | bytes 27656 | tf_op jit(solution)/shard_map/ppermute | solution.py:33
  277.3 2.3 collective-permute-start.16
  279.6 3.3 %collective-permute-done.16 = bf16[18,1,256]{2,1,0:T(2,128)(2,1)S(1)} collective-permute-done((bf16[18,1,256]{2,1,0:T(2,128)(2,1)S(1)}, bf16[18,1,256]{2,1,0:T(2,128)(2,1)S(1)}, u32[]{:S(2)}, u32[]{:S(2)}) %collective-permute-start.16) | collective-permute-done | bytes 9248 | tf_op jit(solution)/shard_map/ppermute | solution.py:32
  (155 shorter events, 66.9 us)
Async XLA Ops:
  6.5 255.2 %copy-start = (bf16[3,3,304,256]{3,2,1,0:T(8,128)(2,1)S(1)}, bf16[3,3,304,256]{3,2,1,0:T(8,128)(2,1)}, u32[]{:S(2)}) copy-start(bf16[3,3,304,256]{3,2,1,0:T(8,128)(2,1)} %param.24) | copy-start | bytes 4202500
  6.5 71.7 %all-gather.2.cloned.1.call-start = ((), (), s32[]{:S(2)}) async-start(), calls=%async_computation.1 | async-start | bytes 6684672 | tf_op jit(solution)/shard_map/all_gather | solution.py:134
  88.0 10.8 %copy-start.17 = (bf16[3,3,3,2048,16]{3,4,2,1,0:T(8,128)(2,1)S(1)}, bf16[3,3,3,2048,16]{3,4,2,1,0:T(8,128)(2,1)}, u32[]{:S(2)}) copy-start(bf16[3,3,3,2048,16]{3,4,2,1,0:T(8,128)(2,1)} %param.17) | copy-start | bytes 5308420
  88.0 10.8 %copy-start.19 = (bf16[2048,16]{0,1:T(8,128)(2,1)S(1)}, bf16[2048,16]{0,1:T(8,128)(2,1)}, u32[]{:S(2)}) copy-start(bf16[2048,16]{0,1:T(8,128)(2,1)} %param.16) | copy-start | bytes 196612
  158.6 26.0 %copy-start.2 = (f32[128,12,16]{2,1,0:T(8,128)S(1)}, f32[128,12,16]{2,1,0:T(8,128)}, u32[]{:S(2)}) copy-start(f32[128,12,16]{2,1,0:T(8,128)} %get-tuple-element.31) | copy-start | bytes 294916
  164.0 30.6 %copy-start.10 = (f32[128,12,16]{0,2,1:T(8,128)S(1)}, f32[128,12,16]{0,2,1:T(8,128)}, u32[]{:S(2)}) copy-start(f32[128,12,16]{0,2,1:T(8,128)} %copy.223) | copy-start | bytes 294916
  164.0 32.4 %copy-start.8 = (f32[128,12,16]{0,2,1:T(8,128)S(1)}, f32[128,12,16]{0,2,1:T(8,128)}, u32[]{:S(2)}) copy-start(f32[128,12,16]{0,2,1:T(8,128)} %copy.224) | copy-start | bytes 294916
  164.0 32.4 %copy-start.9 = (f32[128,12,16]{0,2,1:T(8,128)S(1)}, f32[128,12,16]{0,2,1:T(8,128)}, u32[]{:S(2)}) copy-start(f32[128,12,16]{0,2,1:T(8,128)} %copy.225) | copy-start | bytes 294916
  164.0 32.4 %collective-permute-start.5 = (f32[128,12,16]{0,2,1:T(8,128)}, f32[128,12,16]{0,2,1:T(8,128)}, u32[]{:S(2)}, u32[]{:S(2)}) collective-permute-start(f32[128,12,16]{0,2,1:T(8,128)} %copy.197), channel_id=1, source_target_pairs={{3,0},{4,1},{5,2},{6,3},{7,4},{11,8},{12,9},{13,10},{14,11},{15,12... | collective-permute-start | bytes 294920 | tf_op jit(solution)/shard_map/ppermute | solution.py:16
  165.4 20.1 %collective-permute-start.1 = (f32[128,12,16]{0,2,1:T(8,128)}, f32[128,12,16]{0,2,1:T(8,128)S(1)}, u32[]{:S(2)}, u32[]{:S(2)}) collective-permute-start(f32[128,12,16]{0,2,1:T(8,128)} %copy.187), channel_id=1, source_target_pairs={{1,0},{2,1},{3,2},{4,3},{5,4},{6,5},{7,6},{9,8},{10,9},{11,10},{12... | collective-permute-start | bytes 294920 | tf_op jit(solution)/shard_map/ppermute | solution.py:16
  167.8 24.2 %collective-permute-start.2 = (f32[128,12,16]{0,2,1:T(8,128)}, f32[128,12,16]{0,2,1:T(8,128)}, u32[]{:S(2)}, u32[]{:S(2)}) collective-permute-start(f32[128,12,16]{0,2,1:T(8,128)} %copy.188), channel_id=1, source_target_pairs={{0,2},{1,3},{2,4},{3,5},{4,6},{5,7},{8,10},{9,11},{10,12},{11,13},... | collective-permute-start | bytes 294920 | tf_op jit(solution)/shard_map/ppermute | solution.py:16
  174.4 22.0 %collective-permute-start.4 = (f32[128,12,16]{0,2,1:T(8,128)}, f32[128,12,16]{0,2,1:T(8,128)}, u32[]{:S(2)}, u32[]{:S(2)}) collective-permute-start(f32[128,12,16]{0,2,1:T(8,128)} %copy.193), channel_id=1, source_target_pairs={{0,3},{1,4},{2,5},{3,6},{4,7},{8,11},{9,12},{10,13},{11,14},{12,15... | collective-permute-start | bytes 294920 | tf_op jit(solution)/shard_map/ppermute | solution.py:16
  181.1 8.3 %collective-permute-start = (f32[128,12,16]{0,2,1:T(8,128)}, f32[128,12,16]{0,2,1:T(8,128)S(1)}, u32[]{:S(2)}, u32[]{:S(2)}) collective-permute-start(f32[128,12,16]{0,2,1:T(8,128)} %copy.183), channel_id=1, source_target_pairs={{0,1},{1,2},{2,3},{3,4},{4,5},{5,6},{6,7},{8,9},{9,10},{10,11},{11... | collective-permute-start | bytes 294920 | tf_op jit(solution)/shard_map/ppermute | solution.py:16
  185.6 9.1 %collective-permute-start.3 = (f32[128,12,16]{0,2,1:T(8,128)}, f32[128,12,16]{0,2,1:T(8,128)S(1)}, u32[]{:S(2)}, u32[]{:S(2)}) collective-permute-start(f32[128,12,16]{0,2,1:T(8,128)} %copy.192), channel_id=1, source_target_pairs={{2,0},{3,1},{4,2},{5,3},{6,4},{7,5},{10,8},{11,9},{12,10},{13,11},... | collective-permute-start | bytes 294920 | tf_op jit(solution)/shard_map/ppermute | solution.py:16
  190.0 17.4 %copy-start.7 = (bf16[1280,256]{1,0:T(8,128)(2,1)S(1)}, bf16[1280,256]{1,0:T(8,128)(2,1)}, u32[]{:S(2)}) copy-start(bf16[1280,256]{1,0:T(8,128)(2,1)} %param.20) | copy-start | bytes 1966084
  201.7 12.0 %all-to-all-start = ((bf16[16,2,3840]{2,1,0:T(2,128)(2,1)}), bf16[16,2,3840]{2,1,0:T(2,128)(2,1)S(1)}, u32[]{:S(2)}, u32[]{:S(2)}) async-start(bf16[16,2,3840]{2,1,0:T(2,128)(2,1)} %reshape.102), calls=%async_computation | async-start | bytes 491520 | tf_op jit(solution)/shard_map/all_to_all | solution.py:177
  207.4 7.7 %copy-start.15 = (f32[256]{0:T(256)S(1)}, f32[256]{0:T(256)}, u32[]{:S(2)}) copy-start(f32[256]{0:T(256)} %param.21) | copy-start | bytes 3076
  207.5 25.2 %copy-start.11 = (bf16[16,24,256]{2,1,0:T(8,128)(2,1)S(1)}, bf16[16,24,256]{2,1,0:T(8,128)(2,1)}, u32[]{:S(2)}) copy-start(bf16[16,24,256]{2,1,0:T(8,128)(2,1)} %param.15) | copy-start | bytes 589828
  207.5 25.2 %copy-start.14 = (bf16[256,48]{0,1:T(8,128)(2,1)S(1)}, bf16[256,48]{0,1:T(8,128)(2,1)}, u32[]{:S(2)}) copy-start(bf16[256,48]{0,1:T(8,128)(2,1)} %param.22) | copy-start | bytes 73732
  207.5 25.2 %copy-start.16 = (f32[48]{0:T(128)S(1)}, f32[48]{0:T(128)}, u32[]{:S(2)}) copy-start(f32[48]{0:T(128)} %param.23) | copy-start | bytes 580
  215.4 5.9 %collective-permute-start.6 = (bf16[1,12,256]{2,1,0:T(8,128)(2,1)S(1)}, bf16[1,12,256]{2,1,0:T(8,128)(2,1)S(1)}, u32[]{:S(2)}, u32[]{:S(2)}) collective-permute-start(bf16[1,12,256]{2,1,0:T(8,128)(2,1)S(1)} %get-tuple-element.77), channel_id=1, source_target_pairs={{0,8},{8,16},{16,24},{24,32},{32,40},{40,48},{48,56},{56,64},{64,7... | collective-permute-start | bytes 18440 | tf_op jit(solution)/shard_map/ppermute | solution.py:32
  219.1 7.7 %collective-permute-start.7 = (bf16[1,12,256]{2,1,0:T(8,128)(2,1)S(1)}, bf16[1,12,256]{2,1,0:T(8,128)(2,1)S(1)}, u32[]{:S(2)}, u32[]{:S(2)}) collective-permute-start(bf16[1,12,256]{2,1,0:T(8,128)(2,1)S(1)} %get-tuple-element.76), channel_id=1, source_target_pairs={{8,0},{16,8},{24,16},{32,24},{40,32},{48,40},{56,48},{64,56},{72,6... | collective-permute-start | bytes 18440 | tf_op jit(solution)/shard_map/ppermute | solution.py:33
  226.8 6.3 %collective-permute-start.8 = (bf16[10,1,256]{2,1,0:T(2,128)(2,1)S(1)}, bf16[10,1,256]{2,1,0:T(2,128)(2,1)S(1)}, u32[]{:S(2)}, u32[]{:S(2)}) collective-permute-start(bf16[10,1,256]{2,1,0:T(2,128)(2,1)S(1)} %get-tuple-element.74), channel_id=1, source_target_pairs={{0,1},{1,2},{2,3},{3,4},{4,5},{5,6},{6,7},{8,9},{9,10},{10,11},{11... | collective-permute-start | bytes 15368 | tf_op jit(solution)/shard_map/ppermute | solution.py:32
  228.7 5.6 %collective-permute-start.9 = (bf16[10,1,256]{2,1,0:T(2,128)(2,1)S(1)}, bf16[10,1,256]{2,1,0:T(2,128)(2,1)S(1)}, u32[]{:S(2)}, u32[]{:S(2)}) collective-permute-start(bf16[10,1,256]{2,1,0:T(2,128)(2,1)S(1)} %get-tuple-element.75), channel_id=1, source_target_pairs={{1,0},{2,1},{3,2},{4,3},{5,4},{6,5},{7,6},{9,8},{10,9},{11,10},{12... | collective-permute-start | bytes 15368 | tf_op jit(solution)/shard_map/ppermute | solution.py:33
  235.1 6.8 %collective-permute-start.10 = (bf16[1,24,304]{2,0,1:T(2,128)(2,1)S(1)}, bf16[1,24,304]{2,0,1:T(2,128)(2,1)S(1)}, u32[]{:S(2)}, u32[]{:S(2)}) collective-permute-start(bf16[1,24,304]{2,0,1:T(2,128)(2,1)S(1)} %get-tuple-element.56), channel_id=1, source_target_pairs={{0,8},{8,16},{16,24},{24,32},{32,40},{40,48},{48,56},{56,64},{64,7... | collective-permute-start | bytes 43784 | tf_op jit(solution)/shard_map/ppermute | solution.py:32
  237.1 8.0 %collective-permute-start.11 = (bf16[1,24,304]{2,0,1:T(2,128)(2,1)S(1)}, bf16[1,24,304]{2,0,1:T(2,128)(2,1)S(1)}, u32[]{:S(2)}, u32[]{:S(2)}) collective-permute-start(bf16[1,24,304]{2,0,1:T(2,128)(2,1)S(1)} %get-tuple-element.57), channel_id=1, source_target_pairs={{8,0},{16,8},{24,16},{32,24},{40,32},{48,40},{56,48},{64,56},{72,6... | collective-permute-start | bytes 43784 | tf_op jit(solution)/shard_map/ppermute | solution.py:33
  245.1 6.5 %collective-permute-start.13 = (bf16[18,1,304]{2,0,1:T(8,128)(2,1)S(1)}, bf16[18,1,304]{2,0,1:T(8,128)(2,1)S(1)}, u32[]{:S(2)}, u32[]{:S(2)}) collective-permute-start(bf16[18,1,304]{2,0,1:T(8,128)(2,1)S(1)} %get-tuple-element.46), channel_id=1, source_target_pairs={{1,0},{2,1},{3,2},{4,3},{5,4},{6,5},{7,6},{9,8},{10,9},{11,10},{12... | collective-permute-start | bytes 32840 | tf_op jit(solution)/shard_map/ppermute | solution.py:33
  249.2 5.7 %collective-permute-start.12 = (bf16[18,1,304]{2,0,1:T(8,128)(2,1)S(1)}, bf16[18,1,304]{2,0,1:T(8,128)(2,1)S(1)}, u32[]{:S(2)}, u32[]{:S(2)}) collective-permute-start(bf16[18,1,304]{2,0,1:T(8,128)(2,1)S(1)} %get-tuple-element.47), channel_id=1, source_target_pairs={{0,1},{1,2},{2,3},{3,4},{4,5},{5,6},{6,7},{8,9},{9,10},{10,11},{11... | collective-permute-start | bytes 32840 | tf_op jit(solution)/shard_map/ppermute | solution.py:32
  264.1 5.9 %collective-permute-start.14 = (bf16[1,24,256]{2,1,0:T(8,128)(2,1)S(1)}, bf16[1,24,256]{2,1,0:T(8,128)(2,1)S(1)}, u32[]{:S(2)}, u32[]{:S(2)}) collective-permute-start(bf16[1,24,256]{2,1,0:T(8,128)(2,1)S(1)} %get-tuple-element.66), channel_id=1, source_target_pairs={{0,8},{8,16},{16,24},{24,32},{32,40},{40,48},{48,56},{56,64},{64,7... | collective-permute-start | bytes 36872 | tf_op jit(solution)/shard_map/ppermute | solution.py:32
  266.0 7.7 %collective-permute-start.15 = (bf16[1,24,256]{2,1,0:T(8,128)(2,1)S(1)}, bf16[1,24,256]{2,1,0:T(8,128)(2,1)S(1)}, u32[]{:S(2)}, u32[]{:S(2)}) collective-permute-start(bf16[1,24,256]{2,1,0:T(8,128)(2,1)S(1)} %get-tuple-element.67), channel_id=1, source_target_pairs={{8,0},{16,8},{24,16},{32,24},{40,32},{48,40},{56,48},{64,56},{72,6... | collective-permute-start | bytes 36872 | tf_op jit(solution)/shard_map/ppermute | solution.py:33
  273.7 5.9 %collective-permute-start.17 = (bf16[18,1,256]{2,1,0:T(2,128)(2,1)S(1)}, bf16[18,1,256]{2,1,0:T(2,128)(2,1)S(1)}, u32[]{:S(2)}, u32[]{:S(2)}) collective-permute-start(bf16[18,1,256]{2,1,0:T(2,128)(2,1)S(1)} %get-tuple-element.62), channel_id=1, source_target_pairs={{1,0},{2,1},{3,2},{4,3},{5,4},{6,5},{7,6},{9,8},{10,9},{11,10},{12... | collective-permute-start | bytes 27656 | tf_op jit(solution)/shard_map/ppermute | solution.py:33
  277.3 5.7 %collective-permute-start.16 = (bf16[18,1,256]{2,1,0:T(2,128)(2,1)S(1)}, bf16[18,1,256]{2,1,0:T(2,128)(2,1)S(1)}, u32[]{:S(2)}, u32[]{:S(2)}) collective-permute-start(bf16[18,1,256]{2,1,0:T(2,128)(2,1)S(1)} %get-tuple-element.63), channel_id=1, source_target_pairs={{0,1},{1,2},{2,3},{3,4},{4,5},{5,6},{6,7},{8,9},{9,10},{10,11},{11... | collective-permute-start | bytes 27656 | tf_op jit(solution)/shard_map/ppermute | solution.py:32
  (10 other events, 24.3 us)
Sparse Core Ops, SparseCore 0:
  9.8 68.4 all-gather.1
where the time goes:
time: 295 us; the launch traced here: 293 us
  local copies, waits for them, and re-layouts  84.3 us (29%)
  starting transfers between devices  63.8 us (22%)
  blocking collectives  60.8 us (21%)
  waiting for transfers between devices  36.8 us (12%)
  other arithmetic  20.4 us (7%)
  between operations  14.2 us (5%)
  matrix products  12.4 us (4%)
    psum x3, blocking collectives, one_axis_at_a_time(): value = lax.psum(value, axis)  60.8 us
    ppermute x6, starting transfers between devices, from_behind(): return lax.ppermute(value, axis, pairs)  22.8 us
    unnamed x66, local copies, waits for them, and re-layouts  22.7 us
    ppermute x6, starting transfers between devices, padded_2(): after = lax.ppermute(first, axis, down)  21.6 us
    ppermute x6, starting transfers between devices, padded_2(): before = lax.ppermute(last, axis, up)  13.6 us
    slice x1, local copies, waits for them, and re-layouts, group(): return products[:, :, number * own_width:(number + 1) * own_width]  13.5 us
    ppermute x6, waiting for transfers between devices, padded_2(): after = lax.ppermute(first, axis, down)  13.4 us
    reshape x1, local copies, waits for them, and re-layouts, on_device(): piece.reshape(-1, in_width)  10.8 us
  transfers between devices with their start and end apart: 20, of which 9 were waited for; matrix products, arithmetic and copies ran while one was open for 4% of the time, Pallas kernels for 0%

commit v1 on v0

--- a/solution.py
+++ b/solution.py
@@ -131,7 +131,8 @@
     own_stack = jnp.concatenate([point_weight, atrous_flat, pool_weight], axis=1)
     group_total = 28
     stacked = own_stack[:, : group_total * own_width]
-    piece = lax.all_gather(features, ROW, axis=0, tiled=True)
+    repeated = jnp.stack([features] * lax.axis_size(ROW))
+    piece = jnp.concatenate(lax.all_to_all(repeated, ROW, 0, 0), axis=0)
     result = jnp.dot(piece.reshape(-1, in_width), stacked, preferred_element_type=jnp.float32)
     products = result.reshape(piece.shape[0], piece.shape[1], -1)
     map_rows = products.shape[0]

time: 295 us -> 351 us (1.19)
  blocking collectives: 60.8 us -> 128 us
  between operations: 14.2 us -> 0.81 us
  waiting for transfers between devices: 36.8 us -> 26.6 us
  starting transfers between devices: 63.8 us -> 72.9 us
  local copies, waits for them, and re-layouts: 84.3 us -> 90.7 us
    psum x3, blocking collectives: 60.8 us -> 128 us  [one_axis_at_a_time(): value = lax.psum(value, axis)]
    another operation x0 -> x2, local copies, waits for them, and re-layouts: none -> 15.4 us  [the longest x1 10.8 us: on_device(): piece.reshape(-1, in_width)]
    all_to_all x0 -> x1, local copies, waits for them, and re-layouts: none -> 11.5 us  [on_device(): piece = jnp.concatenate(lax.all_to_all(repeated, ROW, 0, 0), axis=0)]
    reshape x1 -> x0, local copies, waits for them, and re-layouts: 10.8 us -> none  [on_device(): piece.reshape(-1, in_width)]
    all_gather x1 -> x0, local copies, waits for them, and re-layouts: 9.74 us -> none  [on_device(): piece = lax.all_gather(features, ROW, axis=0, tiled=True)]
    all_to_all x0 -> x1, starting transfers between devices: none -> 7.55 us  [on_device(): piece = jnp.concatenate(lax.all_to_all(repeated, ROW, 0, 0), axis=0)]
    all_gather x1 -> x0, waiting for transfers between devices: 7.23 us -> none  [on_device(): piece = lax.all_gather(features, ROW, axis=0, tiled=True)]
    unnamed x66 -> x72, local copies, waits for them, and re-layouts: 22.7 us -> 22.7 us
  transfers between devices with their start and end apart: 20 -> 20, of which waited for: 9 -> 8; matrix products, arithmetic and copies ran while one was open for 4% -> 2% of each run, Pallas kernels for 0% -> 0%
where the time goes in v1:
time: 351 us; the launch traced here: 349 us
  blocking collectives  128 us (36%)
  local copies, waits for them, and re-layouts  90.7 us (26%)
  starting transfers between devices  72.9 us (21%)
  waiting for transfers between devices  26.6 us (8%)
  other arithmetic  18.6 us (5%)
  matrix products  11.6 us (3%)
    psum x3, blocking collectives, one_axis_at_a_time(): value = lax.psum(value, axis)  128 us
    ppermute x6, starting transfers between devices, from_behind(): return lax.ppermute(value, axis, pairs)  22.8 us
    unnamed x72, local copies, waits for them, and re-layouts  22.7 us
    ppermute x6, starting transfers between devices, padded_2(): after = lax.ppermute(first, axis, down)  20.3 us
    ppermute x6, starting transfers between devices, padded_2(): before = lax.ppermute(last, axis, up)  15 us
    ppermute x6, waiting for transfers between devices, padded_2(): after = lax.ppermute(first, axis, down)  13.5 us
    slice x1, local copies, waits for them, and re-layouts, group(): return products[:, :, number * own_width:(number + 1) * own_width]  13.5 us
    all_to_all x1, local copies, waits for them, and re-layouts, on_device(): piece = jnp.concatenate(lax.all_to_all(repeated, ROW, 0, 0), axis=0)  11.5 us
  transfers between devices with their start and end apart: 20, of which 8 were waited for; matrix products, arithmetic and copies ran while one was open for 2% of the time, Pallas kernels for 0%

profile of v1, /device:TPU:70, one launch (start us, length us, event | category | flops | bytes accessed | tf_op | source)
XLA Modules:
  0.0 349.2 jit_solution(13149293095165722410)
XLA Ops:
  0.0 4.6 %stack.14 = bf16[16,8,12,2048]{3,1,2,0:T(8,128)(2,1)} broadcast(bf16[8,12,2048]{2,0,1:T(8,128)(2,1)} %param.14), dimensions={1,2,3} | broadcast | bytes 6684672 | tf_op jit(solution)/shard_map/stack | solution.py:134
  4.6 7.6 %all-to-all-start = ((bf16[16,8,12,2048]{3,1,2,0:T(8,128)(2,1)}), bf16[16,8,12,2048]{3,1,2,0:T(8,128)(2,1)}, u32[]{:S(2)}, u32[]{:S(2)}) async-start(bf16[16,8,12,2048]{3,1,2,0:T(8,128)(2,1)} %stack.14), calls=%async_computation | async-start | bytes 12582912 | tf_op jit(solution)/shard_map/all_to_all | solution.py:135
  12.6 79.6 %all-reduce.20 = (f32[5,256]{1,0:T(8,128)S(1)}, f32[2048]{0:T(1024)S(1)}) all-reduce(f32[5,256]{1,0:T(8,128)S(1)} %dynamic_update_slice.3, f32[2048]{0:T(1024)S(1)} %convert_reduce_fusion), channel_id=1, replica_groups=mesh['dp'=2,'row_0'=4,'row_1'=4,'col'=8] {'row_0'}, use_global_device_ids=true, to_apply=%region_0.1 | all-reduce | flops 3328 | bytes 26624 | tf_op jit(solution)/shard_map/psum | solution.py:21
  92.2 18.8 %all-reduce.19 = (f32[5,256]{1,0:T(8,128)S(1)}, f32[2048]{0:T(1024)S(1)}) all-reduce(f32[5,256]{1,0:T(8,128)S(1)} %get-tuple-element.9, f32[2048]{0:T(1024)S(1)} %get-tuple-element.10), channel_id=1, replica_groups=mesh['dp'=2,'row_0'=4,'row_1'=4,'col'=8] {'row_1'}, use_global_device_ids=true, to_apply=%region_1.2 | all-reduce | flops 3328 | bytes 26624 | tf_op jit(solution)/shard_map/psum | solution.py:21
  110.9 29.7 %all-reduce.18 = (f32[5,256]{1,0:T(8,128)S(1)}, f32[2048]{0:T(1024)S(1)}) all-reduce(f32[5,256]{1,0:T(8,128)S(1)} %get-tuple-element.7, f32[2048]{0:T(1024)S(1)} %get-tuple-element.8), channel_id=1, replica_groups=mesh['dp'=2,'row_0'=4,'row_1'=4,'col'=8] {'col'}, use_global_device_ids=true, to_apply=%region_2.3 | all-reduce | flops 3328 | bytes 26624 | tf_op jit(solution)/shard_map/psum | solution.py:21
  140.9 11.5 %copy.181 = bf16[16,8,12,2048]{3,2,1,0:T(8,128)(2,1)} copy(bf16[16,8,12,2048]{3,1,2,0:T(8,128)(2,1)} %all-to-all-done) | data formatting | bytes 12582912 | tf_op jit(solution)/shard_map/all_to_all | solution.py:135
  152.3 10.8 %reshape_reshape.3 = bf16[1536,2048]{1,0:T(8,128)(2,1)} reshape(bf16[16,8,12,2048]{3,2,1,0:T(8,128)(2,1)} %copy.181) | data formatting | bytes 12582912 | tf_op jit(solution)/shard_map/reshape;reshape | solution.py:136
  163.2 7.3 %convolution_bitcast_fusion = f32[1536,448]{0,1:T(8,128)} fusion(bf16[1536,2048]{1,0:T(8,128)(2,1)} %reshape_reshape.3, bf16[2048,432]{0,1:T(8,128)(2,1)S(1)} %bitcast.118, bf16[2048,16]{0,1:T(8,128)(2,1)S(1)} %copy-done.22), kind=kOutput, calls=%fused_computation | convolution fusion | flops 2822242304 | bytes 10878976 | tf_op jit(solution)/shard_map/dot_general | solution.py:136
  170.5 3.5 copy.182
  174.0 4.6 %reshape.86 = f32[128,12,448]{2,1,0:T(8,128)} reshape(f32[1536,448]{1,0:T(8,128)} %copy.182) | data formatting | bytes 5505024 | tf_op jit(solution)/shard_map/reshape | solution.py:137
  178.6 13.5 %fusion.61 = (f32[128,12,16]{2,1,0:T(8,128)}, f32[128,12,16]{2,1,0:T(8,128)}, f32[128,12,16]{2,1,0:T(8,128)}, f32[128,12,16]{2,1,0:T(8,128)}, f32[128,12,16]{2,1...) fusion(f32[128,12,448]{2,1,0:T(8,128)} %reshape.86), kind=kLoop, calls=%fused_computation.144 | loop fusion | bytes 3735552 | tf_op jit(solution)/shard_map/slice | solution.py:141
  202.8 2.2 copy.221
  209.3 8.6 %fusion.62 = (f32[128,12,16]{2,1,0:T(8,128)}, f32[128,12,16]{2,1,0:T(8,128)}, f32[128,12,16]{2,1,0:T(8,128)}, f32[128,12,16]{2,1,0:T(8,128)}, f32[128,12,16]{2,1...) fusion(f32[128,12,448]{2,1,0:T(8,128)} %reshape.86, ...), kind=kLoop, calls=%fused_computation.145 | loop fusion | flops 245760 | bytes 2555904 | tf_op jit(solution)/shard_map/slice | solution.py:141
  222.8 2.2 copy.189
  231.5 9.3 %collective-permute-start.2 = (f32[128,12,16]{0,2,1:T(8,128)}, f32[128,12,16]{0,2,1:T(8,128)}, u32[]{:S(2)}, u32[]{:S(2)}) collective-permute-start(f32[128,12,16]{0,2,1:T(8,128)} %copy.189), channel_id=1, source_target_pairs={{0,2},{1,3},{2,4},{3,5},{4,6},{5,7},{8,10},{9,11},{10,12},{11,13},... | collective-permute-start | bytes 294920 | tf_op jit(solution)/shard_map/ppermute | solution.py:16
  240.8 2.7 collective-permute-start.4
  248.0 5.6 %collective-permute-start.3 = (f32[128,12,16]{0,2,1:T(8,128)}, f32[128,12,16]{0,2,1:T(8,128)S(1)}, u32[]{:S(2)}, u32[]{:S(2)}) collective-permute-start(f32[128,12,16]{0,2,1:T(8,128)} %copy.193), channel_id=1, source_target_pairs={{2,0},{3,1},{4,2},{5,3},{6,4},{7,5},{10,8},{11,9},{12,10},{13,11},... | collective-permute-start | bytes 294920 | tf_op jit(solution)/shard_map/ppermute | solution.py:16
  264.9 7.3 %all-to-all-start.1 = ((bf16[16,2,3840]{2,1,0:T(2,128)(2,1)}), bf16[16,2,3840]{2,1,0:T(2,128)(2,1)S(1)}, u32[]{:S(2)}, u32[]{:S(2)}) async-start(bf16[16,2,3840]{2,1,0:T(2,128)(2,1)} %reshape.100), calls=%async_computation.1 | async-start | bytes 491520 | tf_op jit(solution)/shard_map/all_to_all | solution.py:178
  272.2 6.2 %all-to-all-done.1 = bf16[16,2,3840]{2,1,0:T(2,128)(2,1)S(1)} async-done(((bf16[16,2,3840]{2,1,0:T(2,128)(2,1)}), bf16[16,2,3840]{2,1,0:T(2,128)(2,1)S(1)}, u32[]{:S(2)}, u32[]{:S(2)}) %all-to-all-start.1) | async-done | bytes 245792 | tf_op jit(solution)/shard_map/all_to_all | solution.py:178
  280.2 3.6 %collective-permute-start.6 = (bf16[1,12,256]{2,1,0:T(8,128)(2,1)S(1)}, bf16[1,12,256]{2,1,0:T(8,128)(2,1)S(1)}, u32[]{:S(2)}, u32[]{:S(2)}) collective-permute-start(bf16[1,12,256]{2,1,0:T(8,128)(2,1)S(1)} %get-tuple-element.77), channel_id=1, source_target_pairs={{0,8},{8,16},{16,24},{24,32},{32,40},{40,48},{48,56},{56,64},{64,7... | collective-permute-start | bytes 18440 | tf_op jit(solution)/shard_map/ppermute | solution.py:32
  283.8 2.2 collective-permute-start.7
  286.1 5.5 %collective-permute-done.7 = bf16[1,12,256]{2,1,0:T(8,128)(2,1)S(1)} collective-permute-done((bf16[1,12,256]{2,1,0:T(8,128)(2,1)S(1)}, bf16[1,12,256]{2,1,0:T(8,128)(2,1)S(1)}, u32[]{:S(2)}, u32[]{:S(2)}) %collective-permute-start.7) | collective-permute-done | bytes 6176 | tf_op jit(solution)/shard_map/ppermute | solution.py:33
  293.5 3.9 %collective-permute-start.9 = (bf16[10,1,256]{2,1,0:T(2,128)(2,1)S(1)}, bf16[10,1,256]{2,1,0:T(2,128)(2,1)S(1)}, u32[]{:S(2)}, u32[]{:S(2)}) collective-permute-start(bf16[10,1,256]{2,1,0:T(2,128)(2,1)S(1)} %get-tuple-element.75), channel_id=1, source_target_pairs={{1,0},{2,1},{3,2},{4,3},{5,4},{6,5},{7,6},{9,8},{10,9},{11,10},{12... | collective-permute-start | bytes 15368 | tf_op jit(solution)/shard_map/ppermute | solution.py:33
  301.8 3.9 %collective-permute-start.11 = (bf16[1,24,304]{2,0,1:T(2,128)(2,1)S(1)}, bf16[1,24,304]{2,0,1:T(2,128)(2,1)S(1)}, u32[]{:S(2)}, u32[]{:S(2)}) collective-permute-start(bf16[1,24,304]{2,0,1:T(2,128)(2,1)S(1)} %get-tuple-element.57), channel_id=1, source_target_pairs={{8,0},{16,8},{24,16},{32,24},{40,32},{48,40},{56,48},{64,56},{72,6... | collective-permute-start | bytes 43784 | tf_op jit(solution)/shard_map/ppermute | solution.py:33
  306.7 3.1 collective-permute-done.11
  309.8 4.1 %collective-permute-start.13 = (bf16[18,1,304]{2,0,1:T(8,128)(2,1)S(1)}, bf16[18,1,304]{2,0,1:T(8,128)(2,1)S(1)}, u32[]{:S(2)}, u32[]{:S(2)}) collective-permute-start(bf16[18,1,304]{2,0,1:T(8,128)(2,1)S(1)} %get-tuple-element.46), channel_id=1, source_target_pairs={{1,0},{2,1},{3,2},{4,3},{5,4},{6,5},{7,6},{9,8},{10,9},{11,10},{12... | collective-permute-start | bytes 32840 | tf_op jit(solution)/shard_map/ppermute | solution.py:33
  316.3 3.3 collective-permute-done.12
  321.5 4.9 %concatenate.122 = bf16[384,2736]{1,0:T(8,128)(2,1)} concatenate(bf16[384,304]{1,0:T(8,128)(2,1)S(1)} %bitcast.104, bf16[384,304]{1,0:T(8,128)(2,1)S(1)} %bitcast.100, bf16[384,304]{1,0:T(8,128)(2,1)S(1)} %bitcast.103, bf16[384,304]{1,0:T(8,128)(2,1)S(1)} %bitcast.105, bf16[384,256]{1,0:T(8,128)(2,1)} %convert_element_type.76, bf16[384,48]{1,0:T(8,128)(2,1)} %copy-done.7, ...), dimensions={1} | concatenate | bytes 4202496 | tf_op jit(solution)/shard_map/concatenate | solution.py:61
  326.5 2.3 fusion.6
  330.8 3.9 %collective-permute-start.15 = (bf16[1,24,256]{2,1,0:T(8,128)(2,1)S(1)}, bf16[1,24,256]{2,1,0:T(8,128)(2,1)S(1)}, u32[]{:S(2)}, u32[]{:S(2)}) collective-permute-start(bf16[1,24,256]{2,1,0:T(8,128)(2,1)S(1)} %get-tuple-element.67), channel_id=1, source_target_pairs={{8,0},{16,8},{24,16},{32,24},{40,32},{48,40},{56,48},{64,56},{72,6... | collective-permute-start | bytes 36872 | tf_op jit(solution)/shard_map/ppermute | solution.py:33
  334.7 3.8 %collective-permute-done.15 = bf16[1,24,256]{2,1,0:T(8,128)(2,1)S(1)} collective-permute-done((bf16[1,24,256]{2,1,0:T(8,128)(2,1)S(1)}, bf16[1,24,256]{2,1,0:T(8,128)(2,1)S(1)}, u32[]{:S(2)}, u32[]{:S(2)}) %collective-permute-start.15) | collective-permute-done | bytes 12320 | tf_op jit(solution)/shard_map/ppermute | solution.py:33
  340.7 3.7 %collective-permute-start.16 = (bf16[18,1,256]{2,1,0:T(2,128)(2,1)S(1)}, bf16[18,1,256]{2,1,0:T(2,128)(2,1)S(1)}, u32[]{:S(2)}, u32[]{:S(2)}) collective-permute-start(bf16[18,1,256]{2,1,0:T(2,128)(2,1)S(1)} %get-tuple-element.63), channel_id=1, source_target_pairs={{0,1},{1,2},{2,3},{3,4},{4,5},{5,6},{6,7},{8,9},{9,10},{10,11},{11... | collective-permute-start | bytes 27656 | tf_op jit(solution)/shard_map/ppermute | solution.py:32
  (161 shorter events, 64.8 us)
Async XLA Ops:
  0.0 326.5 %copy-start = (bf16[3,3,304,256]{3,2,1,0:T(8,128)(2,1)S(1)}, bf16[3,3,304,256]{3,2,1,0:T(8,128)(2,1)}, u32[]{:S(2)}) copy-start(bf16[3,3,304,256]{3,2,1,0:T(8,128)(2,1)} %param.24) | copy-start | bytes 4202500
  4.6 136.1 %copy-start.21 = (bf16[2048,16]{0,1:T(8,128)(2,1)S(1)}, bf16[2048,16]{0,1:T(8,128)(2,1)}, u32[]{:S(2)}) copy-start(bf16[2048,16]{0,1:T(8,128)(2,1)} %param.18) | copy-start | bytes 196612
  4.6 136.3 %all-to-all-start = ((bf16[16,8,12,2048]{3,1,2,0:T(8,128)(2,1)}), bf16[16,8,12,2048]{3,1,2,0:T(8,128)(2,1)}, u32[]{:S(2)}, u32[]{:S(2)}) async-start(bf16[16,8,12,2048]{3,1,2,0:T(8,128)(2,1)} %stack.14), calls=%async_computation | async-start | bytes 12582912 | tf_op jit(solution)/shard_map/all_to_all | solution.py:135
  152.3 10.8 %copy-start.19 = (bf16[3,3,3,2048,16]{3,4,2,1,0:T(8,128)(2,1)S(1)}, bf16[3,3,3,2048,16]{3,4,2,1,0:T(8,128)(2,1)}, u32[]{:S(2)}) copy-start(bf16[3,3,3,2048,16]{3,4,2,1,0:T(8,128)(2,1)} %param.17) | copy-start | bytes 5308420
  152.3 10.8 %copy-start.22 = (bf16[2048,16]{0,1:T(8,128)(2,1)S(1)}, bf16[2048,16]{0,1:T(8,128)(2,1)}, u32[]{:S(2)}) copy-start(bf16[2048,16]{0,1:T(8,128)(2,1)} %param.16) | copy-start | bytes 196612
  222.8 24.2 %copy-start.2 = (f32[128,12,16]{2,1,0:T(8,128)S(1)}, f32[128,12,16]{2,1,0:T(8,128)}, u32[]{:S(2)}) copy-start(f32[128,12,16]{2,1,0:T(8,128)} %get-tuple-element.31) | copy-start | bytes 294916
  228.1 29.7 %copy-start.11 = (f32[128,12,16]{0,2,1:T(8,128)S(1)}, f32[128,12,16]{0,2,1:T(8,128)}, u32[]{:S(2)}) copy-start(f32[128,12,16]{0,2,1:T(8,128)} %copy.224) | copy-start | bytes 294916
  228.1 31.5 %copy-start.9 = (f32[128,12,16]{0,2,1:T(8,128)S(1)}, f32[128,12,16]{0,2,1:T(8,128)}, u32[]{:S(2)}) copy-start(f32[128,12,16]{0,2,1:T(8,128)} %copy.225) | copy-start | bytes 294916
  228.1 31.5 %copy-start.10 = (f32[128,12,16]{0,2,1:T(8,128)S(1)}, f32[128,12,16]{0,2,1:T(8,128)}, u32[]{:S(2)}) copy-start(f32[128,12,16]{0,2,1:T(8,128)} %copy.226) | copy-start | bytes 294916
  228.1 31.5 %collective-permute-start.5 = (f32[128,12,16]{0,2,1:T(8,128)}, f32[128,12,16]{0,2,1:T(8,128)}, u32[]{:S(2)}, u32[]{:S(2)}) collective-permute-start(f32[128,12,16]{0,2,1:T(8,128)} %copy.198), channel_id=1, source_target_pairs={{3,0},{4,1},{5,2},{6,3},{7,4},{11,8},{12,9},{13,10},{14,11},{15,12... | collective-permute-start | bytes 294920 | tf_op jit(solution)/shard_map/ppermute | solution.py:16
  229.5 18.4 %collective-permute-start.1 = (f32[128,12,16]{0,2,1:T(8,128)}, f32[128,12,16]{0,2,1:T(8,128)S(1)}, u32[]{:S(2)}, u32[]{:S(2)}) collective-permute-start(f32[128,12,16]{0,2,1:T(8,128)} %copy.188), channel_id=1, source_target_pairs={{1,0},{2,1},{3,2},{4,3},{5,4},{6,5},{7,6},{9,8},{10,9},{11,10},{12... | collective-permute-start | bytes 294920 | tf_op jit(solution)/shard_map/ppermute | solution.py:16
  231.5 24.6 %collective-permute-start.2 = (f32[128,12,16]{0,2,1:T(8,128)}, f32[128,12,16]{0,2,1:T(8,128)}, u32[]{:S(2)}, u32[]{:S(2)}) collective-permute-start(f32[128,12,16]{0,2,1:T(8,128)} %copy.189), channel_id=1, source_target_pairs={{0,2},{1,3},{2,4},{3,5},{4,6},{5,7},{8,10},{9,11},{10,12},{11,13},... | collective-permute-start | bytes 294920 | tf_op jit(solution)/shard_map/ppermute | solution.py:16
  240.8 18.8 %collective-permute-start.4 = (f32[128,12,16]{0,2,1:T(8,128)}, f32[128,12,16]{0,2,1:T(8,128)}, u32[]{:S(2)}, u32[]{:S(2)}) collective-permute-start(f32[128,12,16]{0,2,1:T(8,128)} %copy.194), channel_id=1, source_target_pairs={{0,3},{1,4},{2,5},{3,6},{4,7},{8,11},{9,12},{10,13},{11,14},{12,15... | collective-permute-start | bytes 294920 | tf_op jit(solution)/shard_map/ppermute | solution.py:16
  243.4 10.1 %collective-permute-start = (f32[128,12,16]{0,2,1:T(8,128)}, f32[128,12,16]{0,2,1:T(8,128)S(1)}, u32[]{:S(2)}, u32[]{:S(2)}) collective-permute-start(f32[128,12,16]{0,2,1:T(8,128)} %copy.184), channel_id=1, source_target_pairs={{0,1},{1,2},{2,3},{3,4},{4,5},{5,6},{6,7},{8,9},{9,10},{10,11},{11... | collective-permute-start | bytes 294920 | tf_op jit(solution)/shard_map/ppermute | solution.py:16
  248.0 9.9 %collective-permute-start.3 = (f32[128,12,16]{0,2,1:T(8,128)}, f32[128,12,16]{0,2,1:T(8,128)S(1)}, u32[]{:S(2)}, u32[]{:S(2)}) collective-permute-start(f32[128,12,16]{0,2,1:T(8,128)} %copy.193), channel_id=1, source_target_pairs={{2,0},{3,1},{4,2},{5,3},{6,4},{7,5},{10,8},{11,9},{12,10},{13,11},... | collective-permute-start | bytes 294920 | tf_op jit(solution)/shard_map/ppermute | solution.py:16
  254.2 17.9 %copy-start.8 = (bf16[1280,256]{1,0:T(8,128)(2,1)S(1)}, bf16[1280,256]{1,0:T(8,128)(2,1)}, u32[]{:S(2)}) copy-start(bf16[1280,256]{1,0:T(8,128)(2,1)} %param.20) | copy-start | bytes 1966084
  264.9 13.5 %all-to-all-start.1 = ((bf16[16,2,3840]{2,1,0:T(2,128)(2,1)}), bf16[16,2,3840]{2,1,0:T(2,128)(2,1)S(1)}, u32[]{:S(2)}, u32[]{:S(2)}) async-start(bf16[16,2,3840]{2,1,0:T(2,128)(2,1)} %reshape.100), calls=%async_computation.1 | async-start | bytes 491520 | tf_op jit(solution)/shard_map/all_to_all | solution.py:178
  272.2 25.2 %copy-start.12 = (bf16[16,24,256]{2,1,0:T(8,128)(2,1)S(1)}, bf16[16,24,256]{2,1,0:T(8,128)(2,1)}, u32[]{:S(2)}) copy-start(bf16[16,24,256]{2,1,0:T(8,128)(2,1)} %param.15) | copy-start | bytes 589828
  272.2 25.2 %copy-start.15 = (bf16[256,48]{0,1:T(8,128)(2,1)S(1)}, bf16[256,48]{0,1:T(8,128)(2,1)}, u32[]{:S(2)}) copy-start(bf16[256,48]{0,1:T(8,128)(2,1)} %param.22) | copy-start | bytes 73732
  272.2 25.2 %copy-start.18 = (f32[48]{0:T(128)S(1)}, f32[48]{0:T(128)}, u32[]{:S(2)}) copy-start(f32[48]{0:T(128)} %param.23) | copy-start | bytes 580
  280.2 5.9 %collective-permute-start.6 = (bf16[1,12,256]{2,1,0:T(8,128)(2,1)S(1)}, bf16[1,12,256]{2,1,0:T(8,128)(2,1)S(1)}, u32[]{:S(2)}, u32[]{:S(2)}) collective-permute-start(bf16[1,12,256]{2,1,0:T(8,128)(2,1)S(1)} %get-tuple-element.77), channel_id=1, source_target_pairs={{0,8},{8,16},{16,24},{24,32},{32,40},{40,48},{48,56},{56,64},{64,7... | collective-permute-start | bytes 18440 | tf_op jit(solution)/shard_map/ppermute | solution.py:32
  283.8 7.7 %collective-permute-start.7 = (bf16[1,12,256]{2,1,0:T(8,128)(2,1)S(1)}, bf16[1,12,256]{2,1,0:T(8,128)(2,1)S(1)}, u32[]{:S(2)}, u32[]{:S(2)}) collective-permute-start(bf16[1,12,256]{2,1,0:T(8,128)(2,1)S(1)} %get-tuple-element.76), channel_id=1, source_target_pairs={{8,0},{16,8},{24,16},{32,24},{40,32},{48,40},{56,48},{64,56},{72,6... | collective-permute-start | bytes 18440 | tf_op jit(solution)/shard_map/ppermute | solution.py:33
  291.6 6.3 %collective-permute-start.8 = (bf16[10,1,256]{2,1,0:T(2,128)(2,1)S(1)}, bf16[10,1,256]{2,1,0:T(2,128)(2,1)S(1)}, u32[]{:S(2)}, u32[]{:S(2)}) collective-permute-start(bf16[10,1,256]{2,1,0:T(2,128)(2,1)S(1)} %get-tuple-element.74), channel_id=1, source_target_pairs={{0,1},{1,2},{2,3},{3,4},{4,5},{5,6},{6,7},{8,9},{9,10},{10,11},{11... | collective-permute-start | bytes 15368 | tf_op jit(solution)/shard_map/ppermute | solution.py:32
  293.5 5.6 %collective-permute-start.9 = (bf16[10,1,256]{2,1,0:T(2,128)(2,1)S(1)}, bf16[10,1,256]{2,1,0:T(2,128)(2,1)S(1)}, u32[]{:S(2)}, u32[]{:S(2)}) collective-permute-start(bf16[10,1,256]{2,1,0:T(2,128)(2,1)S(1)} %get-tuple-element.75), channel_id=1, source_target_pairs={{1,0},{2,1},{3,2},{4,3},{5,4},{6,5},{7,6},{9,8},{10,9},{11,10},{12... | collective-permute-start | bytes 15368 | tf_op jit(solution)/shard_map/ppermute | solution.py:33
  299.9 6.8 %collective-permute-start.10 = (bf16[1,24,304]{2,0,1:T(2,128)(2,1)S(1)}, bf16[1,24,304]{2,0,1:T(2,128)(2,1)S(1)}, u32[]{:S(2)}, u32[]{:S(2)}) collective-permute-start(bf16[1,24,304]{2,0,1:T(2,128)(2,1)S(1)} %get-tuple-element.56), channel_id=1, source_target_pairs={{0,8},{8,16},{16,24},{24,32},{32,40},{40,48},{48,56},{56,64},{64,7... | collective-permute-start | bytes 43784 | tf_op jit(solution)/shard_map/ppermute | solution.py:32
  301.8 8.0 %collective-permute-start.11 = (bf16[1,24,304]{2,0,1:T(2,128)(2,1)S(1)}, bf16[1,24,304]{2,0,1:T(2,128)(2,1)S(1)}, u32[]{:S(2)}, u32[]{:S(2)}) collective-permute-start(bf16[1,24,304]{2,0,1:T(2,128)(2,1)S(1)} %get-tuple-element.57), channel_id=1, source_target_pairs={{8,0},{16,8},{24,16},{32,24},{40,32},{48,40},{56,48},{64,56},{72,6... | collective-permute-start | bytes 43784 | tf_op jit(solution)/shard_map/ppermute | solution.py:33
  309.8 6.5 %collective-permute-start.13 = (bf16[18,1,304]{2,0,1:T(8,128)(2,1)S(1)}, bf16[18,1,304]{2,0,1:T(8,128)(2,1)S(1)}, u32[]{:S(2)}, u32[]{:S(2)}) collective-permute-start(bf16[18,1,304]{2,0,1:T(8,128)(2,1)S(1)} %get-tuple-element.46), channel_id=1, source_target_pairs={{1,0},{2,1},{3,2},{4,3},{5,4},{6,5},{7,6},{9,8},{10,9},{11,10},{12... | collective-permute-start | bytes 32840 | tf_op jit(solution)/shard_map/ppermute | solution.py:33
  314.0 5.7 %collective-permute-start.12 = (bf16[18,1,304]{2,0,1:T(8,128)(2,1)S(1)}, bf16[18,1,304]{2,0,1:T(8,128)(2,1)S(1)}, u32[]{:S(2)}, u32[]{:S(2)}) collective-permute-start(bf16[18,1,304]{2,0,1:T(8,128)(2,1)S(1)} %get-tuple-element.47), channel_id=1, source_target_pairs={{0,1},{1,2},{2,3},{3,4},{4,5},{5,6},{6,7},{8,9},{9,10},{10,11},{11... | collective-permute-start | bytes 32840 | tf_op jit(solution)/shard_map/ppermute | solution.py:32
  328.8 5.9 %collective-permute-start.14 = (bf16[1,24,256]{2,1,0:T(8,128)(2,1)S(1)}, bf16[1,24,256]{2,1,0:T(8,128)(2,1)S(1)}, u32[]{:S(2)}, u32[]{:S(2)}) collective-permute-start(bf16[1,24,256]{2,1,0:T(8,128)(2,1)S(1)} %get-tuple-element.66), channel_id=1, source_target_pairs={{0,8},{8,16},{16,24},{24,32},{32,40},{40,48},{48,56},{56,64},{64,7... | collective-permute-start | bytes 36872 | tf_op jit(solution)/shard_map/ppermute | solution.py:32
  330.8 7.7 %collective-permute-start.15 = (bf16[1,24,256]{2,1,0:T(8,128)(2,1)S(1)}, bf16[1,24,256]{2,1,0:T(8,128)(2,1)S(1)}, u32[]{:S(2)}, u32[]{:S(2)}) collective-permute-start(bf16[1,24,256]{2,1,0:T(8,128)(2,1)S(1)} %get-tuple-element.67), channel_id=1, source_target_pairs={{8,0},{16,8},{24,16},{32,24},{40,32},{48,40},{56,48},{64,56},{72,6... | collective-permute-start | bytes 36872 | tf_op jit(solution)/shard_map/ppermute | solution.py:33
  338.5 5.9 %collective-permute-start.17 = (bf16[18,1,256]{2,1,0:T(2,128)(2,1)S(1)}, bf16[18,1,256]{2,1,0:T(2,128)(2,1)S(1)}, u32[]{:S(2)}, u32[]{:S(2)}) collective-permute-start(bf16[18,1,256]{2,1,0:T(2,128)(2,1)S(1)} %get-tuple-element.62), channel_id=1, source_target_pairs={{1,0},{2,1},{3,2},{4,3},{5,4},{6,5},{7,6},{9,8},{10,9},{11,10},{12... | collective-permute-start | bytes 27656 | tf_op jit(solution)/shard_map/ppermute | solution.py:33
  340.7 5.7 %collective-permute-start.16 = (bf16[18,1,256]{2,1,0:T(2,128)(2,1)S(1)}, bf16[18,1,256]{2,1,0:T(2,128)(2,1)S(1)}, u32[]{:S(2)}, u32[]{:S(2)}) collective-permute-start(bf16[18,1,256]{2,1,0:T(2,128)(2,1)S(1)} %get-tuple-element.63), channel_id=1, source_target_pairs={{0,1},{1,2},{2,3},{3,4},{4,5},{5,6},{6,7},{8,9},{9,10},{10,11},{11... | collective-permute-start | bytes 27656 | tf_op jit(solution)/shard_map/ppermute | solution.py:32
  (13 other events, 49.2 us)
